TPU v7x, 256 devices: a whole 4x4x8 slice. The times are simulated.
256 devices in a mesh: req: 8 (over z_lo, core), tile: 16 (over x, y), blk: 2 (over z_hi).
Axes of the slice: x: 4, y: 4, z: 8 (z_hi: 2, z_lo: 4; z = z_hi * 4 + z_lo), core: 2. Of those that a mesh axis runs over, the one named last changes fastest.
Arguments:
- image_tokens: bfloat16 [16, 1024, 1536], P(('req', 'blk'), 'tile'), may hold values from -6 to 6
- latent: float32 [16, 512, 128], P(('req', 'blk'), 'tile'), may hold values from -6 to 6
- modulation: float32 [16, 8, 1536], P(('req', 'blk')), may hold values from -3 to 3
- text_kv: bfloat16 [16, 154, 2, 1536], P(('req', 'blk')), as said below
- text_len: int32 [16], P(('req', 'blk')), may hold values from 38 to 154, as said below
- timestep: int32 [16], P(('req', 'blk')), may hold values from 0 to 7
- w_qkv: bfloat16 [1536, 3, 1536], P(None, None, 'tile'), may hold values from -0.15625 to 0.15625
- w_out: bfloat16 [1536, 1536], P('tile'), may hold values from -0.15625 to 0.15625
- w_up: bfloat16 [1536, 6144], P(None, 'tile'), may hold values from -0.15625 to 0.15625
- w_down: bfloat16 [6144, 1536], P('tile'), may hold values from -0.078125 to 0.078125
- w_final: bfloat16 [1536, 64], replicated, may hold values from -0.15625 to 0.15625
Outputs:
- image_state: bfloat16 [16, 1024, 1536], P(('req', 'blk'), 'tile')
- latent_next: float32 [16, 512, 128], P(('req', 'blk'), 'tile')
Inputs may be any that keep to these rules, and one draw needn't show every extreme that they name: `text_len`: each request has 38 to 154 live text tokens; some request has 154 and some 154 // 4. `text_kv`: keys and values of text tokens, finite.
All inputs are finite; a program needn't handle non-finite values.
Results may differ from a plain program's by a relative error of at most 0.014.
Values may be sent and summed in bfloat16 or wider, within the bound.
No kernel may reach another device: no remote copies, remote signals or barrier semaphores. Data moves between devices by JAX's collectives and lax.ppermute only.
A program may use at most 64 MiB of HBM per device.

v0:
```python
import jax
import jax.numpy as jnp
from jax import lax
from jax.sharding import PartitionSpec as P

HEAD_DIM = 64
TXT = 154
STEPS = 8


def normed(value, shift, scale):
    full = value.astype(jnp.float32)
    mean = jnp.mean(full, axis=-1, keepdims=True)
    spread = jnp.mean(jnp.square(full - mean), axis=-1, keepdims=True)
    return (full - mean) * lax.rsqrt(spread + 1e-06) * (1.0 + scale) + shift


def sigma_at(index):
    frac = 1.0 - index.astype(jnp.float32) / STEPS
    return 3.0 * frac / (1.0 + 2.0 * frac)


def on_device(
    image_tokens,
    latent,
    modulation,
    text_kv,
    text_len,
    timestep,
    w_qkv,
    w_out,
    w_up,
    w_down,
    w_final,
):
    tokens = image_tokens[0]
    mods = modulation[0]
    rows_here = tokens.shape[0]
    width = tokens.shape[1]
    heads = width // HEAD_DIM
    scale_factor = HEAD_DIM ** (-0.5)
    h1 = normed(tokens, mods[0], mods[1]).astype(jnp.bfloat16)
    qkv_all = jnp.einsum(
        "nd,dkc->nkc",
        lax.all_gather(h1, "tile", axis=0, tiled=True),
        w_qkv,
        preferred_element_type=jnp.float32,
    ).astype(jnp.bfloat16)
    qkv = lax.all_to_all(qkv_all, "tile", split_axis=0, concat_axis=2, tiled=True)
    query = qkv[:, 0].reshape(rows_here, heads, HEAD_DIM)
    keyval = qkv[:, 1:]
    text_pair = text_kv[0]
    text_keys = text_pair[:, 0].reshape(TXT, heads, HEAD_DIM)
    text_values = text_pair[:, 1].reshape(TXT, heads, HEAD_DIM)
    live = jnp.arange(TXT, dtype=jnp.int32) < text_len[0]
    text_scores = (
        jnp.einsum("qhe,khe->hqk", query, text_keys, preferred_element_type=jnp.float32)
        * scale_factor
    )
    text_scores = jnp.where(live[None, None, :], text_scores, -jnp.inf)
    top_start = jnp.max(text_scores, axis=-1)
    text_weights = jnp.exp(text_scores - top_start[:, :, None])
    total_start = jnp.sum(text_weights, axis=-1)
    acc_start = jnp.einsum(
        "hqk,khe->hqe",
        text_weights.astype(jnp.bfloat16),
        text_values,
        preferred_element_type=jnp.float32,
    )
    piece = lax.all_gather(keyval, "tile", axis=0, tiled=True)
    total = total_start
    acc = acc_start
    count = piece.shape[0]
    piece_keys = piece[:, 0].reshape(count, heads, HEAD_DIM)
    piece_values = piece[:, 1].reshape(count, heads, HEAD_DIM)
    scores = (
        jnp.einsum("qhe,khe->hqk", query, piece_keys, preferred_element_type=jnp.float32)
        * scale_factor
    )
    new_top = jnp.maximum(top_start, jnp.max(scores, axis=-1))
    factor = jnp.exp(top_start - new_top)
    weights = jnp.exp(scores - new_top[:, :, None])
    total = total * factor + jnp.sum(weights, axis=-1)
    acc = acc * factor[:, :, None] + jnp.einsum(
        "hqk,khe->hqe",
        weights.astype(jnp.bfloat16),
        piece_values,
        preferred_element_type=jnp.float32,
    )
    summed = acc / total[:, :, None]
    attended = jnp.transpose(summed, (1, 0, 2)).reshape(rows_here, width).astype(jnp.bfloat16)
    columns = lax.all_to_all(attended, "tile", split_axis=1, concat_axis=0, tiled=True)
    block_rows = columns
    proj = lax.psum_scatter(
        jnp.dot(block_rows, w_out, preferred_element_type=jnp.float32).astype(jnp.bfloat16),
        "tile",
        scatter_dimension=0,
        tiled=True,
    ).astype(jnp.float32)
    second = (tokens.astype(jnp.float32) + mods[2] * proj).astype(jnp.bfloat16)
    h2 = normed(second, mods[3], mods[4]).astype(jnp.bfloat16)
    hidden = jax.nn.gelu(
        jnp.dot(
            lax.all_gather(h2, "tile", axis=0, tiled=True), w_up, preferred_element_type=jnp.float32
        ),
        approximate=True,
    ).astype(jnp.bfloat16)
    block_rows = hidden
    ffn = lax.psum_scatter(
        jnp.dot(block_rows, w_down, preferred_element_type=jnp.float32).astype(jnp.bfloat16),
        "tile",
        scatter_dimension=0,
        tiled=True,
    ).astype(jnp.float32)
    state = (second.astype(jnp.float32) + mods[5] * ffn).astype(jnp.bfloat16)
    final_in = normed(state, mods[6], mods[7]).astype(jnp.bfloat16)
    velocity = jnp.dot(final_in, w_final, preferred_element_type=jnp.float32)
    step_index = timestep[0]
    delta = sigma_at(step_index + 1) - sigma_at(step_index)
    moved = latent[0] + delta * velocity.reshape(rows_here // 2, 2 * velocity.shape[1])
    return (state[None], moved[None])


def solution(mesh):
    in_specs = (
        P(("req", "blk"), "tile", None),
        P(("req", "blk"), "tile", None),
        P(("req", "blk"), None, None),
        P(("req", "blk"), None, None, None),
        P(("req", "blk")),
        P(("req", "blk")),
        P(None, None, "tile"),
        P("tile", None),
        P(None, "tile"),
        P("tile", None),
        P(),
    )
    out_specs = (P(("req", "blk"), "tile", None), P(("req", "blk"), "tile", None))
    return jax.shard_map(
        on_device, mesh=mesh, in_specs=in_specs, out_specs=out_specs, check_vma=False
    )
```

profile of v0, /device:TPU:32, one launch (start us, length us, event | category | flops | bytes accessed | tf_op | source)
XLA Modules:
  0.0 429.9 jit_solution(14177773688961563732)
XLA Ops:
  7.2 0.0 copy-start
  7.2 0.0 all-gather.4.cloned.1.call-start
  7.2 1.4 add_reduce_fusion
  8.6 1.1 convert_reduce_fusion.2
  9.7 1.2 fusion.46
  10.8 1.8 fusion.49
  12.6 0.0 all-gather.4.cloned.1.call-update
  12.6 0.0 all-gather.6.cloned.1.call-start
  12.7 55.7 %all-gather.4.cloned.1.call-done = bf16[1024,1536]{1,0:T(8,128)(2,1)} async-done(((bf16[64,1536]{1,0:T(8,128)(2,1)}), bf16[1024,1536]{1,0:T(8,128)(2,1)}) %all-gather.4.cloned.1.call-update) | async-done | bytes 3145744 | tf_op jit(solution)/shard_map/all_gather | solution.py:45
  68.3 3.2 fusion.74
  71.6 0.1 convert_element_type.71
  71.7 0.7 copy.25
  72.4 20.9 %all_to_all.34 = bf16[1024,3,96]{2,1,0:T(4,128)(2,1)S(1)} all-to-all(bf16[1024,3,96]{2,1,0:T(4,128)(2,1)S(1)} %copy.25), channel_id=1, replica_groups=mesh['req'=8,'tile'=16,'blk'=2] {'tile'}, dimensions={0} | all-to-all | bytes 1179648 | tf_op jit(solution)/shard_map/all_to_all | solution.py:49
  93.3 0.1 copy.26
  93.4 0.5 copy.27
  94.0 0.9 all_to_all.28
  94.9 0.0 copy-start.4
  94.9 0.9 slice.67
  95.7 0.0 all-gather.6.cloned.1.call-update
  95.8 0.0 reduce-scatter.3.cloned.1.call-start
  95.8 0.1 copy-done.4
  95.9 2.1 fusion.70
  98.0 3.1 copy.28
  101.8 1.9 copy.30
  103.7 0.0 slice-done
  103.7 0.2 reshape_squeeze.15
  103.9 1.6 fusion.71
  105.5 0.5 fusion.14
  106.0 54.2 %all-gather.6.cloned.1.call-done = bf16[1024,2,1536]{2,0,1:T(8,128)(2,1)} async-done(((bf16[64,2,1536]{2,0,1:T(8,128)(2,1)}), bf16[1024,2,1536]{2,0,1:T(8,128)(2,1)}) %all-gather.6.cloned.1.call-update) | async-done | bytes 6291472 | tf_op jit(solution)/shard_map/all_gather | solution.py:70
  160.2 5.9 %fusion.69 = (bf16[1024,1,1536]{2,0,1:T(8,128)(2,1)}, bf16[1024,1,1536]{2,0,1:T(8,128)(2,1)}) fusion(bf16[1024,2,1536]{2,0,1:T(8,128)(2,1)} %all-gather.6.cloned.1.call-done), kind=kLoop, calls=%fused_computation.94 | loop fusion | bytes 12582912 | tf_op jit(solution)/shard_map/slice | solution.py:74
  166.1 4.6 %copy.33 = bf16[1024,1,1536]{0,2,1:T(8,128)(2,1)} copy(bf16[1024,1,1536]{2,0,1:T(8,128)(2,1)} %get-tuple-element.17) | data formatting | bytes 6291456 | tf_op jit(solution)/shard_map/slice | solution.py:75
  170.8 4.7 %copy.31 = bf16[1024,1,1536]{0,2,1:T(8,128)(2,1)} copy(bf16[1024,1,1536]{2,0,1:T(8,128)(2,1)} %get-tuple-element.16) | data formatting | bytes 6291456 | tf_op jit(solution)/shard_map/slice | solution.py:74
  175.5 2.9 multiply_reduce_fusion
  178.4 1.3 fusion
  179.8 0.5 copy-done.1
  180.3 1.6 fusion.16
  181.9 0.0 copy-done.5
  181.9 0.0 copy-start.7
  181.9 0.8 fusion.22
  182.8 0.3 copy.34
  183.0 0.2 convert_element_type.75
  183.3 0.1 copy.35
  183.4 13.6 %all_to_all.35 = bf16[64,16,96]{2,0,1:T(8,128)(2,1)S(1)} all-to-all(bf16[64,16,96]{2,0,1:T(8,128)(2,1)S(1)} %copy.35), channel_id=1, replica_groups=mesh['req'=8,'tile'=16,'blk'=2] {'tile'}, dimensions={1} | all-to-all | bytes 393216 | tf_op jit(solution)/shard_map/all_to_all | solution.py:92
  196.9 2.6 convolution_convert_fusion.1
  199.6 0.0 reduce-scatter.3.cloned.1.call-update
  199.6 0.0 all-gather.8.cloned.1.call-start
  199.7 79.1 %reduce-scatter.3.cloned.1.call-done = bf16[64,1536]{1,0:T(8,128)(2,1)} async-done(((bf16[1024,1536]{1,0:T(8,128)(2,1)}), bf16[64,1536]{1,0:T(8,128)(2,1)}) %reduce-scatter.3.cloned.1.call-update) | async-done | bytes 196624 | tf_op jit(solution)/shard_map/reduce_scatter | solution.py:94
  278.7 0.0 copy-done.3
  278.7 1.1 convert_reduce_fusion
  279.8 0.2 fusion.38
  280.1 0.8 fusion.41
  280.9 0.0 all-gather.8.cloned.1.call-update
  280.9 0.0 reduce-scatter.5.cloned.1.call-start
  281.0 52.9 %all-gather.8.cloned.1.call-done = bf16[1024,1536]{1,0:T(8,128)(2,1)} async-done(((bf16[64,1536]{1,0:T(8,128)(2,1)}), bf16[1024,1536]{1,0:T(8,128)(2,1)}) %all-gather.8.cloned.1.call-update) | async-done | bytes 3145744 | tf_op jit(solution)/shard_map/all_gather | solution.py:104
  333.9 7.2 %convolution_convert_fusion = bf16[1024,1536]{1,0:T(8,128)(2,1)} fusion(bf16[384,1536]{1,0:T(8,128)(2,1)S(1)} %copy-done, bf16[1024,1536]{1,0:T(8,128)(2,1)} %all-gather.8.cloned.1.call-done, bf16[1536,384]{1,0:T(8,128)(2,1)S(1)} %copy-done.9), kind=kOutput, calls=%fused_computation.4 | convolution fusion | flops 2421030912 | bytes 8650752 | tf_op jit(solution)/shard_map/dot_general | solution.py:110
  341.1 0.0 reduce-scatter.5.cloned.1.call-update
  341.9 79.1 %reduce-scatter.5.cloned.1.call-done = bf16[64,1536]{1,0:T(8,128)(2,1)} async-done(((bf16[1024,1536]{1,0:T(8,128)(2,1)}), bf16[64,1536]{1,0:T(8,128)(2,1)}) %reduce-scatter.5.cloned.1.call-update) | async-done | bytes 196624 | tf_op jit(solution)/shard_map/reduce_scatter | solution.py:109
  421.1 1.1 convert_reduce_fusion.1
  422.2 0.0 copy-start.6
  422.2 0.2 fusion.42
  422.4 0.3 convolution_multiply_fusion
  422.7 0.1 mul.192
  422.8 0.0 copy-done.8
  422.8 0.6 add.157
  (23 shorter events, 0.1 us)
Async XLA Ops:
  7.2 326.8 %copy-start = (bf16[384,1536]{1,0:T(8,128)(2,1)S(1)}, bf16[384,1536]{1,0:T(8,128)(2,1)}, u32[]{:S(2)}) copy-start(bf16[384,1536]{1,0:T(8,128)(2,1)} %param.20) | copy-start | bytes 3538948
  7.2 61.2 %all-gather.4.cloned.1.call-start = ((), (), s32[]{:S(2)}) async-start(), calls=%async_computation.4 | async-start | bytes 3342336 | tf_op jit(solution)/shard_map/all_gather | solution.py:45
  12.6 147.6 %all-gather.6.cloned.1.call-start = ((), (), s32[]{:S(2)}) async-start(), calls=%async_computation.5 | async-start | bytes 6684672 | tf_op jit(solution)/shard_map/all_gather | solution.py:70
  93.3 2.6 copy-start.2
  94.9 1.1 copy-start.4
  95.8 183.0 %reduce-scatter.3.cloned.1.call-start = ((), (), s32[]{:S(2)}) async-start(), calls=%async_computation.6 | async-start | bytes 3342336 | tf_op jit(solution)/shard_map/reduce_scatter | solution.py:94
  95.9 7.8 %slice-start = ((bf16[64,3,1536]{2,0,1:T(8,128)(2,1)}), bf16[64,1,1536]{2,0,1:T(8,128)(2,1)S(1)}, s32[]{:S(2)}) async-start(bf16[64,3,1536]{2,0,1:T(8,128)(2,1)} %copy-done.4), calls=%async_computation.9 | async-start | bytes 393216 | tf_op jit(solution)/shard_map/slice | solution.py:50
  178.4 1.9 copy-start.1
  180.3 1.6 copy-start.5
  181.9 15.0 %copy-start.7 = (bf16[96,1536]{1,0:T(8,128)(2,1)S(1)}, bf16[96,1536]{1,0:T(8,128)(2,1)}, u32[]{:S(2)}) copy-start(bf16[96,1536]{1,0:T(8,128)(2,1)} %param.18) | copy-start | bytes 884740
  196.9 81.8 %copy-start.3 = (bf16[1,64,1536]{2,1,0:T(8,128)(2,1)S(1)}, bf16[1,64,1536]{2,1,0:T(8,128)(2,1)}, u32[]{:S(2)}) copy-start(bf16[1,64,1536]{2,1,0:T(8,128)(2,1)} %param.11) | copy-start | bytes 589828
  199.6 134.3 %copy-start.9 = (bf16[1536,384]{1,0:T(8,128)(2,1)S(1)}, bf16[1536,384]{1,0:T(8,128)(2,1)}, u32[]{:S(2)}) copy-start(bf16[1536,384]{1,0:T(8,128)(2,1)} %param.19) | copy-start | bytes 3538948
  199.6 134.3 %all-gather.8.cloned.1.call-start = ((), (), s32[]{:S(2)}) async-start(), calls=%async_computation.7 | async-start | bytes 3342336 | tf_op jit(solution)/shard_map/all_gather | solution.py:104
  280.9 140.1 %reduce-scatter.5.cloned.1.call-start = ((), (), s32[]{:S(2)}) async-start(), calls=%async_computation.8 | async-start | bytes 3342336 | tf_op jit(solution)/shard_map/reduce_scatter | solution.py:109
  341.1 81.3 %copy-start.10 = (bf16[1536,64]{0,1:T(8,128)(2,1)S(1)}, bf16[1536,64]{0,1:T(8,128)(2,1)}, u32[]{:S(2)}) copy-start(bf16[1536,64]{0,1:T(8,128)(2,1)} %param.21) | copy-start | bytes 589828
  341.1 81.7 %copy-start.8 = (f32[1,32,128]{2,1,0:T(8,128)S(1)}, f32[1,32,128]{2,1,0:T(8,128)}, u32[]{:S(2)}) copy-start(f32[1,32,128]{2,1,0:T(8,128)} %param.12) | copy-start | bytes 49156
  422.2 1.2 copy-start.6
Sparse Core Ops, SparseCore 0:
  12.7 55.5 all-gather.3
  95.9 64.2 all-gather.5
  199.7 78.9 reduce-scatter.2
  281.6 52.2 all-gather.7
  341.3 79.7 reduce-scatter.4
where the time goes:
time: 431 us; the launch traced here: 430 us
  waiting for transfers between devices  321 us (74%)
  blocking collectives  34.5 us (8%)
  local copies, waits for them, and re-layouts  27 us (6%)
  matrix products  20.2 us (5%)
  between operations  15.4 us (4%)
  other arithmetic  11.4 us (3%)
    reduce_scatter x1, waiting for transfers between devices, on_device(): lax.psum_scatter(jnp.dot(block_rows, w_down, preferred_element_type=jnp.f...  79.1 us
    reduce_scatter x1, waiting for transfers between devices, on_device(): lax.psum_scatter(jnp.dot(block_rows, w_out, preferred_element_type=jnp.fl...  79.1 us
    all_gather x1, waiting for transfers between devices, on_device(): lax.all_gather(h1, 'tile', axis=0, tiled=True)  55.7 us
    all_gather x1, waiting for transfers between devices, on_device(): piece = lax.all_gather(keyval, 'tile', axis=0, tiled=True)  54.2 us
    all_gather x1, waiting for transfers between devices, on_device(): lax.all_gather(h2, 'tile', axis=0, tiled=True)  52.9 us
    all_to_all x1, blocking collectives, on_device(): lax.all_to_all(qkv_all, 'tile', split_axis=0, concat_axis=2, tiled=True)  20.9 us
    all_to_all x1, blocking collectives, on_device(): lax.all_to_all(attended, 'tile', split_axis=1, concat_axis=0, tiled=True)  13.6 us
    slice x2, local copies, waits for them, and re-layouts, on_device(): piece_keys = piece[:, 0].reshape(count, heads, HEAD_DIM)  10.6 us
  transfers between devices with their start and end apart: 5, of which 5 were waited for; matrix products, arithmetic and copies ran while one was open for 2% of the time, Pallas kernels for 0%

commit v1 on v0

--- a/solution.py
+++ b/solution.py
@@ -6,6 +6,31 @@
 HEAD_DIM = 64
 TXT = 154
 STEPS = 8
+
+
+def _shape_group(along_dim, comm_axis, buf):
+    v_now = lax.axis_size(comm_axis)
+    kept_arr = lax.axis_index(comm_axis)
+    all_values, work_now, met_up = (v_now, kept_arr, buf.shape[along_dim])
+    so_far_all = [(dev, (dev + 1) % all_values) for dev in range(all_values)]
+    history = [(dev, (dev - 1) % all_values) for dev in range(all_values)]
+    upper = jnp.zeros(
+        (*buf.shape[:along_dim], all_values * met_up, *buf.shape[along_dim + 1 :]), buf.dtype
+    )
+    upper = lax.dynamic_update_slice_in_dim(upper, buf, work_now * met_up, axis=along_dim)
+    main = x_next = buf
+    seen_now = all_values // 2
+    for j in range(1, seen_now + 1):
+        main = lax.ppermute(main, comm_axis, so_far_all)
+        upper = lax.dynamic_update_slice_in_dim(
+            upper, main, (work_now - j) % all_values * met_up, axis=along_dim
+        )
+        if j < all_values - seen_now:
+            x_next = lax.ppermute(x_next, comm_axis, history)
+            upper = lax.dynamic_update_slice_in_dim(
+                upper, x_next, (work_now + j) % all_values * met_up, axis=along_dim
+            )
+    return upper
 
 
 def normed(value, shift, scale):
@@ -42,7 +67,7 @@
     h1 = normed(tokens, mods[0], mods[1]).astype(jnp.bfloat16)
     qkv_all = jnp.einsum(
         "nd,dkc->nkc",
-        lax.all_gather(h1, "tile", axis=0, tiled=True),
+        _shape_group(0, comm_axis="tile", buf=h1),
         w_qkv,
         preferred_element_type=jnp.float32,
     ).astype(jnp.bfloat16)

time: 431 us -> 451 us (1.046)
  starting transfers between devices: 0.21 us -> 38.1 us
  waiting for transfers between devices: 321 us -> 294 us
  local copies, waits for them, and re-layouts: 27 us -> 40.9 us
  blocking collectives: 34.5 us -> 29.1 us
    all_gather x1 -> x0, waiting for transfers between devices: 55.7 us -> none  [on_device(): lax.all_gather(h1, 'tile', axis=0, tiled=True)]
    ppermute x0 -> x15, starting transfers between devices: none -> 37.7 us  [the longest x7 36.1 us: _shape_group(): x_next = lax.ppermute(x_next, comm_axis, history)]
    ppermute x0 -> x15, waiting for transfers between devices: none -> 28 us  [the longest x8 28 us: _shape_group(): main = lax.ppermute(main, comm_axis, so_far_all)]
    dynamic_update_slice x0 -> x15, local copies, waits for them, and re-layouts: none -> 10.3 us  [the longest x8 5.48 us: _shape_group(): lax.dynamic_update_slice_in_dim(upper, main, (work_now - j) % all_values...]
    all_to_all x1, blocking collectives: 20.9 us -> 15.5 us  [on_device(): lax.all_to_all(qkv_all, 'tile', split_axis=0, concat_axis=2, tiled=True)]
  transfers between devices with their start and end apart: 5 -> 19, of which waited for: 5 -> 12; matrix products, arithmetic and copies ran while one was open for 2% -> 4% of each run, Pallas kernels for 0% -> 0%
where the time goes in v1:
time: 451 us; the launch traced here: 450 us
  waiting for transfers between devices  294 us (65%)
  local copies, waits for them, and re-layouts  40.9 us (9%)
  starting transfers between devices  38.1 us (8%)
  blocking collectives  29.1 us (6%)
  matrix products  21.2 us (5%)
  between operations  15.5 us (3%)
  other arithmetic  11.6 us (3%)
    reduce_scatter x1, waiting for transfers between devices, on_device(): lax.psum_scatter(jnp.dot(block_rows, w_down, preferred_element_type=jnp.f...  79.1 us
    reduce_scatter x1, waiting for transfers between devices, on_device(): lax.psum_scatter(jnp.dot(block_rows, w_out, preferred_element_type=jnp.fl...  78.8 us
    all_gather x1, waiting for transfers between devices, on_device(): piece = lax.all_gather(keyval, 'tile', axis=0, tiled=True)  54.8 us
    all_gather x1, waiting for transfers between devices, on_device(): lax.all_gather(h2, 'tile', axis=0, tiled=True)  53.1 us
    ppermute x7, starting transfers between devices, _shape_group(): x_next = lax.ppermute(x_next, comm_axis, history)  36.1 us
    ppermute x8, waiting for transfers between devices, _shape_group(): main = lax.ppermute(main, comm_axis, so_far_all)  28 us
    all_to_all x1, blocking collectives, on_device(): lax.all_to_all(qkv_all, 'tile', split_axis=0, concat_axis=2, tiled=True)  15.5 us
    all_to_all x1, blocking collectives, on_device(): lax.all_to_all(attended, 'tile', split_axis=1, concat_axis=0, tiled=True)  13.6 us
  transfers between devices with their start and end apart: 19, of which 12 were waited for; matrix products, arithmetic and copies ran while one was open for 4% of the time, Pallas kernels for 0%

profile of v1, /device:TPU:32, one launch (start us, length us, event | category | flops | bytes accessed | tf_op | source)
XLA Modules:
  0.0 450.3 jit_solution(7710923987586129080)
XLA Ops:
  7.2 2.0 add_reduce_fusion
  9.2 1.1 convert_reduce_fusion.2
  10.3 1.2 fusion.46
  11.4 1.9 broadcast_in_dim.17
  13.3 0.8 constant_dynamic-update-slice_fusion.15
  14.2 1.6 collective-permute-start
  15.7 3.8 collective-permute-start.1
  19.5 4.8 %collective-permute-done = bf16[64,1536]{1,0:T(8,128)(2,1)S(1)} collective-permute-done((bf16[64,1536]{1,0:T(8,128)(2,1)S(1)}, bf16[64,1536]{1,0:T(8,128)(2,1)S(1)}, u32[]{:S(2)}, u32[]{:S(2)}) %collective-permute-start) | collective-permute-done | bytes 196640 | tf_op jit(solution)/shard_map/ppermute | solution.py:24
  24.3 5.3 %collective-permute-start.3 = (bf16[64,1536]{1,0:T(8,128)(2,1)S(1)}, bf16[64,1536]{1,0:T(8,128)(2,1)S(1)}, u32[]{:S(2)}, u32[]{:S(2)}) collective-permute-start(bf16[64,1536]{1,0:T(8,128)(2,1)S(1)} %collective-permute-done.1), channel_id=1, source_target_pairs={{0,30},{2,0},{4,2},{6,4},{8,6},{10,8},{12,10},{14,12},{16,14},{18,... | collective-permute-start | bytes 589832 | tf_op jit(solution)/shard_map/ppermute | solution.py:29
  29.6 0.7 constant_dynamic-update-slice_fusion.14
  30.3 0.7 constant_dynamic-update-slice_fusion.13
  31.0 2.5 collective-permute-done.2
  33.6 5.3 %collective-permute-start.5 = (bf16[64,1536]{1,0:T(8,128)(2,1)S(1)}, bf16[64,1536]{1,0:T(8,128)(2,1)S(1)}, u32[]{:S(2)}, u32[]{:S(2)}) collective-permute-start(bf16[64,1536]{1,0:T(8,128)(2,1)S(1)} %collective-permute-done.3), channel_id=1, source_target_pairs={{0,30},{2,0},{4,2},{6,4},{8,6},{10,8},{12,10},{14,12},{16,14},{18,... | collective-permute-start | bytes 589832 | tf_op jit(solution)/shard_map/ppermute | solution.py:29
  38.9 0.7 constant_dynamic-update-slice_fusion.12
  39.6 0.7 constant_dynamic-update-slice_fusion.11
  40.3 2.3 collective-permute-done.4
  42.5 5.3 %collective-permute-start.7 = (bf16[64,1536]{1,0:T(8,128)(2,1)S(1)}, bf16[64,1536]{1,0:T(8,128)(2,1)S(1)}, u32[]{:S(2)}, u32[]{:S(2)}) collective-permute-start(bf16[64,1536]{1,0:T(8,128)(2,1)S(1)} %collective-permute-done.5), channel_id=1, source_target_pairs={{0,30},{2,0},{4,2},{6,4},{8,6},{10,8},{12,10},{14,12},{16,14},{18,... | collective-permute-start | bytes 589832 | tf_op jit(solution)/shard_map/ppermute | solution.py:29
  47.9 0.7 constant_dynamic-update-slice_fusion.10
  48.6 0.7 constant_dynamic-update-slice_fusion.9
  49.3 2.3 collective-permute-done.6
  51.5 5.3 %collective-permute-start.9 = (bf16[64,1536]{1,0:T(8,128)(2,1)S(1)}, bf16[64,1536]{1,0:T(8,128)(2,1)S(1)}, u32[]{:S(2)}, u32[]{:S(2)}) collective-permute-start(bf16[64,1536]{1,0:T(8,128)(2,1)S(1)} %collective-permute-done.7), channel_id=1, source_target_pairs={{0,30},{2,0},{4,2},{6,4},{8,6},{10,8},{12,10},{14,12},{16,14},{18,... | collective-permute-start | bytes 589832 | tf_op jit(solution)/shard_map/ppermute | solution.py:29
  56.9 0.7 constant_dynamic-update-slice_fusion.8
  57.6 0.7 constant_dynamic-update-slice_fusion.7
  58.2 2.3 collective-permute-done.8
  60.5 5.3 %collective-permute-start.11 = (bf16[64,1536]{1,0:T(8,128)(2,1)S(1)}, bf16[64,1536]{1,0:T(8,128)(2,1)S(1)}, u32[]{:S(2)}, u32[]{:S(2)}) collective-permute-start(bf16[64,1536]{1,0:T(8,128)(2,1)S(1)} %collective-permute-done.9), channel_id=1, source_target_pairs={{0,30},{2,0},{4,2},{6,4},{8,6},{10,8},{12,10},{14,12},{16,14},{18,... | collective-permute-start | bytes 589832 | tf_op jit(solution)/shard_map/ppermute | solution.py:29
  65.9 0.7 constant_dynamic-update-slice_fusion.6
  66.6 0.7 constant_dynamic-update-slice_fusion.5
  67.3 2.7 collective-permute-done.10
  69.9 5.6 %collective-permute-start.13 = (bf16[64,1536]{1,0:T(8,128)(2,1)S(1)}, bf16[64,1536]{1,0:T(8,128)(2,1)S(1)}, u32[]{:S(2)}, u32[]{:S(2)}) collective-permute-start(bf16[64,1536]{1,0:T(8,128)(2,1)S(1)} %collective-permute-done.11), channel_id=1, source_target_pairs={{0,30},{2,0},{4,2},{6,4},{8,6},{10,8},{12,10},{14,12},{16,14},{18,... | collective-permute-start | bytes 589832 | tf_op jit(solution)/shard_map/ppermute | solution.py:29
  75.6 0.7 constant_dynamic-update-slice_fusion.4
  76.2 0.7 constant_dynamic-update-slice_fusion.3
  76.9 3.6 collective-permute-done.12
  80.5 0.7 constant_dynamic-update-slice_fusion.2
  81.2 0.7 constant_dynamic-update-slice_fusion.1
  81.9 7.6 %collective-permute-done.14 = bf16[64,1536]{1,0:T(8,128)(2,1)S(1)} collective-permute-done((bf16[64,1536]{1,0:T(8,128)(2,1)S(1)}, bf16[64,1536]{1,0:T(8,128)(2,1)S(1)}, u32[]{:S(2)}, u32[]{:S(2)}) %collective-permute-start.14) | collective-permute-done | bytes 196640 | tf_op jit(solution)/shard_map/ppermute | solution.py:24
  89.5 0.7 constant_dynamic-update-slice_fusion
  90.2 3.2 fusion.75
  93.5 0.7 copy.25
  94.2 15.5 %all_to_all.34 = bf16[1024,3,96]{2,1,0:T(4,128)(2,1)S(1)} all-to-all(bf16[1024,3,96]{2,1,0:T(4,128)(2,1)S(1)} %copy.25), channel_id=1, replica_groups=mesh['req'=8,'tile'=16,'blk'=2] {'tile'}, dimensions={0} | all-to-all | bytes 1179648 | tf_op jit(solution)/shard_map/all_to_all | solution.py:74
  110.4 1.8 all_to_all.28
  112.1 1.8 slice.67
  114.0 2.1 fusion.71
  116.2 3.1 copy.28
  119.9 1.9 copy.30
  122.6 1.6 fusion.72
  124.7 54.8 %all-gather.3.cloned.1.call-done = bf16[1024,2,1536]{2,0,1:T(8,128)(2,1)} async-done(((bf16[64,2,1536]{2,0,1:T(8,128)(2,1)}), bf16[1024,2,1536]{2,0,1:T(8,128)(2,1)}) %all-gather.3.cloned.1.call-update) | async-done | bytes 6291472 | tf_op jit(solution)/shard_map/all_gather | solution.py:95
  179.5 5.9 %fusion.70 = (bf16[1024,1,1536]{2,0,1:T(8,128)(2,1)}, bf16[1024,1,1536]{2,0,1:T(8,128)(2,1)}) fusion(bf16[1024,2,1536]{2,0,1:T(8,128)(2,1)} %all-gather.3.cloned.1.call-done), kind=kLoop, calls=%fused_computation.110 | loop fusion | bytes 12582912 | tf_op jit(solution)/shard_map/slice | solution.py:99
  185.4 4.6 %copy.33 = bf16[1024,1,1536]{0,2,1:T(8,128)(2,1)} copy(bf16[1024,1,1536]{2,0,1:T(8,128)(2,1)} %get-tuple-element.19) | data formatting | bytes 6291456 | tf_op jit(solution)/shard_map/slice | solution.py:100
  190.0 4.7 %copy.31 = bf16[1024,1,1536]{0,2,1:T(8,128)(2,1)} copy(bf16[1024,1,1536]{2,0,1:T(8,128)(2,1)} %get-tuple-element.18) | data formatting | bytes 6291456 | tf_op jit(solution)/shard_map/slice | solution.py:99
  194.7 2.9 multiply_reduce_fusion
  197.7 1.3 fusion
  199.0 0.5 copy-done.1
  199.6 1.6 fusion.16
  201.2 0.8 fusion.22
  202.6 13.6 %all_to_all.35 = bf16[64,16,96]{2,0,1:T(8,128)(2,1)S(1)} all-to-all(bf16[64,16,96]{2,0,1:T(8,128)(2,1)S(1)} %copy.35), channel_id=1, replica_groups=mesh['req'=8,'tile'=16,'blk'=2] {'tile'}, dimensions={1} | all-to-all | bytes 393216 | tf_op jit(solution)/shard_map/all_to_all | solution.py:117
  216.2 3.6 convolution_convert_fusion.1
  220.1 78.8 %reduce-scatter.3.cloned.1.call-done = bf16[64,1536]{1,0:T(8,128)(2,1)} async-done(((bf16[1024,1536]{1,0:T(8,128)(2,1)}), bf16[64,1536]{1,0:T(8,128)(2,1)}) %reduce-scatter.3.cloned.1.call-update) | async-done | bytes 196624 | tf_op jit(solution)/shard_map/reduce_scatter | solution.py:119
  298.9 1.1 convert_reduce_fusion
  300.3 0.8 fusion.41
  301.2 53.1 %all-gather.5.cloned.1.call-done = bf16[1024,1536]{1,0:T(8,128)(2,1)} async-done(((bf16[64,1536]{1,0:T(8,128)(2,1)}), bf16[1024,1536]{1,0:T(8,128)(2,1)}) %all-gather.5.cloned.1.call-update) | async-done | bytes 3145744 | tf_op jit(solution)/shard_map/all_gather | solution.py:129
  354.3 7.2 %convolution_convert_fusion = bf16[1024,1536]{1,0:T(8,128)(2,1)} fusion(bf16[384,1536]{1,0:T(8,128)(2,1)S(1)} %copy-done, bf16[1024,1536]{1,0:T(8,128)(2,1)} %all-gather.5.cloned.1.call-done, bf16[1536,384]{1,0:T(8,128)(2,1)S(1)} %copy-done.11), kind=kOutput, calls=%fused_computation.4 | convolution fusion | flops 2421030912 | bytes 8650752 | tf_op jit(solution)/shard_map/dot_general | solution.py:135
  362.3 79.1 %reduce-scatter.5.cloned.1.call-done = bf16[64,1536]{1,0:T(8,128)(2,1)} async-done(((bf16[1024,1536]{1,0:T(8,128)(2,1)}), bf16[64,1536]{1,0:T(8,128)(2,1)}) %reduce-scatter.5.cloned.1.call-update) | async-done | bytes 196624 | tf_op jit(solution)/shard_map/reduce_scatter | solution.py:134
  441.4 1.1 convert_reduce_fusion.1
  443.1 0.6 add.318
  (70 shorter events, 4.0 us)
Async XLA Ops:
  7.2 347.1 %copy-start = (bf16[384,1536]{1,0:T(8,128)(2,1)S(1)}, bf16[384,1536]{1,0:T(8,128)(2,1)}, u32[]{:S(2)}) copy-start(bf16[384,1536]{1,0:T(8,128)(2,1)} %param.20) | copy-start | bytes 3538948
  7.2 6.1 %copy-start.3 = (bf16[1,64,1536]{2,1,0:T(8,128)(2,1)S(1)}, bf16[1,64,1536]{2,1,0:T(8,128)(2,1)}, u32[]{:S(2)}) copy-start(bf16[1,64,1536]{2,1,0:T(8,128)(2,1)} %param.11) | copy-start | bytes 589828
  7.2 172.3 %all-gather.3.cloned.1.call-start = ((), (), s32[]{:S(2)}) async-start(), calls=%async_computation.4 | async-start | bytes 6684672 | tf_op jit(solution)/shard_map/all_gather | solution.py:95
  14.2 10.1 %collective-permute-start = (bf16[64,1536]{1,0:T(8,128)(2,1)S(1)}, bf16[64,1536]{1,0:T(8,128)(2,1)S(1)}, u32[]{:S(2)}, u32[]{:S(2)}) collective-permute-start(bf16[64,1536]{1,0:T(8,128)(2,1)S(1)} %get-tuple-element.17), channel_id=1, source_target_pairs={{0,2},{2,4},{4,6},{6,8},{8,10},{10,12},{12,14},{14,16},{16,18},{18... | collective-permute-start | bytes 589832 | tf_op jit(solution)/shard_map/ppermute | solution.py:24
  15.7 8.5 %collective-permute-start.1 = (bf16[64,1536]{1,0:T(8,128)(2,1)S(1)}, bf16[64,1536]{1,0:T(8,128)(2,1)S(1)}, u32[]{:S(2)}, u32[]{:S(2)}) collective-permute-start(bf16[64,1536]{1,0:T(8,128)(2,1)S(1)} %get-tuple-element.17), channel_id=1, source_target_pairs={{0,30},{2,0},{4,2},{6,4},{8,6},{10,8},{12,10},{14,12},{16,14},{18,... | collective-permute-start | bytes 589832 | tf_op jit(solution)/shard_map/ppermute | solution.py:29
  24.3 9.3 %collective-permute-start.2 = (bf16[64,1536]{1,0:T(8,128)(2,1)S(1)}, bf16[64,1536]{1,0:T(8,128)(2,1)S(1)}, u32[]{:S(2)}, u32[]{:S(2)}) collective-permute-start(bf16[64,1536]{1,0:T(8,128)(2,1)S(1)} %collective-permute-done), channel_id=1, source_target_pairs={{0,2},{2,4},{4,6},{6,8},{8,10},{10,12},{12,14},{14,16},{16,18},{18... | collective-permute-start | bytes 589832 | tf_op jit(solution)/shard_map/ppermute | solution.py:24
  24.3 9.3 %collective-permute-start.3 = (bf16[64,1536]{1,0:T(8,128)(2,1)S(1)}, bf16[64,1536]{1,0:T(8,128)(2,1)S(1)}, u32[]{:S(2)}, u32[]{:S(2)}) collective-permute-start(bf16[64,1536]{1,0:T(8,128)(2,1)S(1)} %collective-permute-done.1), channel_id=1, source_target_pairs={{0,30},{2,0},{4,2},{6,4},{8,6},{10,8},{12,10},{14,12},{16,14},{18,... | collective-permute-start | bytes 589832 | tf_op jit(solution)/shard_map/ppermute | solution.py:29
  33.6 9.0 %collective-permute-start.4 = (bf16[64,1536]{1,0:T(8,128)(2,1)S(1)}, bf16[64,1536]{1,0:T(8,128)(2,1)S(1)}, u32[]{:S(2)}, u32[]{:S(2)}) collective-permute-start(bf16[64,1536]{1,0:T(8,128)(2,1)S(1)} %collective-permute-done.2), channel_id=1, source_target_pairs={{0,2},{2,4},{4,6},{6,8},{8,10},{10,12},{12,14},{14,16},{16,18},{18... | collective-permute-start | bytes 589832 | tf_op jit(solution)/shard_map/ppermute | solution.py:24
  33.6 9.0 %collective-permute-start.5 = (bf16[64,1536]{1,0:T(8,128)(2,1)S(1)}, bf16[64,1536]{1,0:T(8,128)(2,1)S(1)}, u32[]{:S(2)}, u32[]{:S(2)}) collective-permute-start(bf16[64,1536]{1,0:T(8,128)(2,1)S(1)} %collective-permute-done.3), channel_id=1, source_target_pairs={{0,30},{2,0},{4,2},{6,4},{8,6},{10,8},{12,10},{14,12},{16,14},{18,... | collective-permute-start | bytes 589832 | tf_op jit(solution)/shard_map/ppermute | solution.py:29
  42.5 9.0 %collective-permute-start.6 = (bf16[64,1536]{1,0:T(8,128)(2,1)S(1)}, bf16[64,1536]{1,0:T(8,128)(2,1)S(1)}, u32[]{:S(2)}, u32[]{:S(2)}) collective-permute-start(bf16[64,1536]{1,0:T(8,128)(2,1)S(1)} %collective-permute-done.4), channel_id=1, source_target_pairs={{0,2},{2,4},{4,6},{6,8},{8,10},{10,12},{12,14},{14,16},{16,18},{18... | collective-permute-start | bytes 589832 | tf_op jit(solution)/shard_map/ppermute | solution.py:24
  42.5 9.0 %collective-permute-start.7 = (bf16[64,1536]{1,0:T(8,128)(2,1)S(1)}, bf16[64,1536]{1,0:T(8,128)(2,1)S(1)}, u32[]{:S(2)}, u32[]{:S(2)}) collective-permute-start(bf16[64,1536]{1,0:T(8,128)(2,1)S(1)} %collective-permute-done.5), channel_id=1, source_target_pairs={{0,30},{2,0},{4,2},{6,4},{8,6},{10,8},{12,10},{14,12},{16,14},{18,... | collective-permute-start | bytes 589832 | tf_op jit(solution)/shard_map/ppermute | solution.py:29
  51.5 9.0 %collective-permute-start.8 = (bf16[64,1536]{1,0:T(8,128)(2,1)S(1)}, bf16[64,1536]{1,0:T(8,128)(2,1)S(1)}, u32[]{:S(2)}, u32[]{:S(2)}) collective-permute-start(bf16[64,1536]{1,0:T(8,128)(2,1)S(1)} %collective-permute-done.6), channel_id=1, source_target_pairs={{0,2},{2,4},{4,6},{6,8},{8,10},{10,12},{12,14},{14,16},{16,18},{18... | collective-permute-start | bytes 589832 | tf_op jit(solution)/shard_map/ppermute | solution.py:24
  51.5 9.0 %collective-permute-start.9 = (bf16[64,1536]{1,0:T(8,128)(2,1)S(1)}, bf16[64,1536]{1,0:T(8,128)(2,1)S(1)}, u32[]{:S(2)}, u32[]{:S(2)}) collective-permute-start(bf16[64,1536]{1,0:T(8,128)(2,1)S(1)} %collective-permute-done.7), channel_id=1, source_target_pairs={{0,30},{2,0},{4,2},{6,4},{8,6},{10,8},{12,10},{14,12},{16,14},{18,... | collective-permute-start | bytes 589832 | tf_op jit(solution)/shard_map/ppermute | solution.py:29
  60.5 9.4 %collective-permute-start.10 = (bf16[64,1536]{1,0:T(8,128)(2,1)S(1)}, bf16[64,1536]{1,0:T(8,128)(2,1)S(1)}, u32[]{:S(2)}, u32[]{:S(2)}) collective-permute-start(bf16[64,1536]{1,0:T(8,128)(2,1)S(1)} %collective-permute-done.8), channel_id=1, source_target_pairs={{0,2},{2,4},{4,6},{6,8},{8,10},{10,12},{12,14},{14,16},{16,18},{18... | collective-permute-start | bytes 589832 | tf_op jit(solution)/shard_map/ppermute | solution.py:24
  60.5 9.4 %collective-permute-start.11 = (bf16[64,1536]{1,0:T(8,128)(2,1)S(1)}, bf16[64,1536]{1,0:T(8,128)(2,1)S(1)}, u32[]{:S(2)}, u32[]{:S(2)}) collective-permute-start(bf16[64,1536]{1,0:T(8,128)(2,1)S(1)} %collective-permute-done.9), channel_id=1, source_target_pairs={{0,30},{2,0},{4,2},{6,4},{8,6},{10,8},{12,10},{14,12},{16,14},{18,... | collective-permute-start | bytes 589832 | tf_op jit(solution)/shard_map/ppermute | solution.py:29
  69.9 10.6 %collective-permute-start.12 = (bf16[64,1536]{1,0:T(8,128)(2,1)S(1)}, bf16[64,1536]{1,0:T(8,128)(2,1)S(1)}, u32[]{:S(2)}, u32[]{:S(2)}) collective-permute-start(bf16[64,1536]{1,0:T(8,128)(2,1)S(1)} %collective-permute-done.10), channel_id=1, source_target_pairs={{0,2},{2,4},{4,6},{6,8},{8,10},{10,12},{12,14},{14,16},{16,18},{18... | collective-permute-start | bytes 589832 | tf_op jit(solution)/shard_map/ppermute | solution.py:24
  69.9 11.3 %collective-permute-start.13 = (bf16[64,1536]{1,0:T(8,128)(2,1)S(1)}, bf16[64,1536]{1,0:T(8,128)(2,1)S(1)}, u32[]{:S(2)}, u32[]{:S(2)}) collective-permute-start(bf16[64,1536]{1,0:T(8,128)(2,1)S(1)} %collective-permute-done.11), channel_id=1, source_target_pairs={{0,30},{2,0},{4,2},{6,4},{8,6},{10,8},{12,10},{14,12},{16,14},{18,... | collective-permute-start | bytes 589832 | tf_op jit(solution)/shard_map/ppermute | solution.py:29
  80.5 9.0 %collective-permute-start.14 = (bf16[64,1536]{1,0:T(8,128)(2,1)S(1)}, bf16[64,1536]{1,0:T(8,128)(2,1)S(1)}, u32[]{:S(2)}, u32[]{:S(2)}) collective-permute-start(bf16[64,1536]{1,0:T(8,128)(2,1)S(1)} %collective-permute-done.12), channel_id=1, source_target_pairs={{0,2},{2,4},{4,6},{6,8},{8,10},{10,12},{12,14},{14,16},{16,18},{18... | collective-permute-start | bytes 589832 | tf_op jit(solution)/shard_map/ppermute | solution.py:24
  109.7 4.3 copy-start.2
  113.9 185.0 %reduce-scatter.3.cloned.1.call-start = ((), (), s32[]{:S(2)}) async-start(), calls=%async_computation.5 | async-start | bytes 3342336 | tf_op jit(solution)/shard_map/reduce_scatter | solution.py:119
  114.0 8.3 %slice-start = ((bf16[64,3,1536]{2,0,1:T(8,128)(2,1)}), bf16[64,1,1536]{2,0,1:T(8,128)(2,1)S(1)}, s32[]{:S(2)}) async-start(bf16[64,3,1536]{2,0,1:T(8,128)(2,1)} %all_to_all.28), calls=%async_computation.8 | async-start | bytes 393216 | tf_op jit(solution)/shard_map/slice | solution.py:75
  197.7 1.9 copy-start.1
  199.6 1.6 copy-start.4
  216.2 84.1 %copy-start.6 = (f32[1536]{0:T(1024)S(1)}, f32[1536]{0:T(1024)}, u32[]{:S(2)}) copy-start(f32[1536]{0:T(1024)} %get-tuple-element.3) | copy-start | bytes 18436
  216.2 84.1 %copy-start.7 = (f32[1536]{0:T(1024)S(1)}, f32[1536]{0:T(1024)}, u32[]{:S(2)}) copy-start(f32[1536]{0:T(1024)} %get-tuple-element.4) | copy-start | bytes 18436
  219.8 134.4 %copy-start.11 = (bf16[1536,384]{1,0:T(8,128)(2,1)S(1)}, bf16[1536,384]{1,0:T(8,128)(2,1)}, u32[]{:S(2)}) copy-start(bf16[1536,384]{1,0:T(8,128)(2,1)} %param.19) | copy-start | bytes 3538948
  219.8 134.4 %all-gather.5.cloned.1.call-start = ((), (), s32[]{:S(2)}) async-start(), calls=%async_computation.6 | async-start | bytes 3342336 | tf_op jit(solution)/shard_map/all_gather | solution.py:129
  301.2 140.2 %reduce-scatter.5.cloned.1.call-start = ((), (), s32[]{:S(2)}) async-start(), calls=%async_computation.7 | async-start | bytes 3342336 | tf_op jit(solution)/shard_map/reduce_scatter | solution.py:134
  361.5 81.3 %copy-start.9 = (f32[1536]{0:T(1024)S(1)}, f32[1536]{0:T(1024)}, u32[]{:S(2)}) copy-start(f32[1536]{0:T(1024)} %get-tuple-element.2) | copy-start | bytes 18436
  361.5 81.3 %copy-start.10 = (f32[1536]{0:T(1024)S(1)}, f32[1536]{0:T(1024)}, u32[]{:S(2)}) copy-start(f32[1536]{0:T(1024)} %get-tuple-element.9) | copy-start | bytes 18436
  361.5 81.3 %copy-start.12 = (bf16[1536,64]{0,1:T(8,128)(2,1)S(1)}, bf16[1536,64]{0,1:T(8,128)(2,1)}, u32[]{:S(2)}) copy-start(bf16[1536,64]{0,1:T(8,128)(2,1)} %param.21) | copy-start | bytes 589828
  361.5 81.7 %copy-start.8 = (f32[1,32,128]{2,1,0:T(8,128)S(1)}, f32[1,32,128]{2,1,0:T(8,128)}, u32[]{:S(2)}) copy-start(f32[1,32,128]{2,1,0:T(8,128)} %param.12) | copy-start | bytes 49156
  442.5 1.2 copy-start.5
Sparse Core Ops, SparseCore 0:
  114.1 65.3 all-gather.2
  220.0 78.9 reduce-scatter.2
  302.0 52.2 all-gather.4
  361.6 79.7 reduce-scatter.4
